TPU v7x, 32 devices: a whole 2x2x4 slice. The times are simulated.
32 devices in a mesh: dp: 8 (over z, y), mp: 4 (over x, core).
Axes of the slice: x: 2, y: 2, z: 4, core: 2. Of those that a mesh axis runs over, the one named last changes fastest.
Arguments:
- tokens: bfloat16 [16560, 1024], P('dp'), may hold values from -6 to 6
- offsets: int32 [48, 5], P('dp'), may hold values from 0 to 308, as said below
- first_gain: float32 [1024], replicated, may hold values from 0.1 to 1.9
- first_shift: float32 [1024], replicated, may hold values from -1.8 to 1.8
- qkv_weight: float32 [1024, 3, 1024], P('dp', None, 'mp'), may hold values from -0.1875 to 0.1875
- qv_bias: float32 [2, 1024], P(None, 'mp'), may hold values from -1.8 to 1.8
- proj_weight: float32 [1024, 1024], P('mp', 'dp'), may hold values from -0.5 to 0.5
- proj_bias: float32 [1024], replicated, may hold values from -1.8 to 1.8
- second_gain: float32 [1024], replicated, may hold values from 0.1 to 1.9
- second_shift: float32 [1024], replicated, may hold values from -1.8 to 1.8
- expand_weight: float32 [1024, 4096], P('dp', 'mp'), may hold values from -0.1875 to 0.1875
- expand_bias: float32 [4096], P('mp'), may hold values from -1.8 to 1.8
- shrink_weight: float32 [4096, 1024], P('mp', 'dp'), may hold values from -0.09375 to 0.09375
- shrink_bias: float32 [1024], replicated, may hold values from -1.8 to 1.8
- cotangent: bfloat16 [16560, 1024], P('dp'), may hold values from -6 to 6
Outputs:
- out: bfloat16 [16560, 1024], P('dp')
- d_tokens: float32 [16560, 1024], P('dp')
- d_first_gain: float32 [1024], replicated
- d_first_shift: float32 [1024], replicated
- d_qkv_weight: float32 [1024, 3, 1024], P('dp', None, 'mp')
- d_qv_bias: float32 [2, 1024], P(None, 'mp')
- d_proj_weight: float32 [1024, 1024], P('mp', 'dp')
- d_proj_bias: float32 [1024], replicated
- d_second_gain: float32 [1024], replicated
- d_second_shift: float32 [1024], replicated
- d_expand_weight: float32 [1024, 4096], P('dp', 'mp')
- d_expand_bias: float32 [4096], P('mp')
- d_shrink_weight: float32 [4096, 1024], P('mp', 'dp')
- d_shrink_bias: float32 [1024], replicated
Inputs may be any that keep to these rules, and one draw needn't show every extreme that they name: `offsets`: each row lists, rising, where the 5 crops of one crop set start within its 345 tokens: the first starts at 0, one crop spans 197 tokens, the others 37 each, and the last ends at the set's end.
All inputs are finite; a program needn't handle non-finite values.
Results may differ from a plain program's by a relative error of at most 0.015.
Values may be sent and summed in bfloat16 or wider, within the bound.
No kernel may reach another device: no remote copies, remote signals or barrier semaphores. Data moves between devices by JAX's collectives and lax.ppermute only.
A program may use at most 128 MiB of HBM per device.

v0:
```python
import jax
import jax.numpy as jnp
from jax import lax
from jax.sharding import PartitionSpec as P

HEAD_DIM = 64
SET_TOKENS = 345
norm_eps = 1e-06
masked_score = -1e30
root_half = 0.7071067811865476


def layer_norm(values, gain, shift):
    centre = jnp.mean(values, axis=-1, keepdims=True)
    offset_rows = values - centre
    spread = jnp.mean(offset_rows * offset_rows, axis=-1, keepdims=True)
    return offset_rows * lax.rsqrt(spread + norm_eps) * gain + shift


def normalized(values):
    centre = jnp.mean(values, axis=-1, keepdims=True)
    offset_rows = values - centre
    spread = jnp.mean(offset_rows * offset_rows, axis=-1, keepdims=True)
    return offset_rows * lax.rsqrt(spread + norm_eps)


def gelu(values):
    return 0.5 * values * (1.0 + lax.erf(values * root_half))


def matmul(left, right):
    return jnp.dot(left, right, preferred_element_type=jnp.float32)


def set_scores(query_rows, key_rows, crop_ids, factor):
    scores = (
        jnp.einsum("qhe,khe->hqk", query_rows, key_rows, preferred_element_type=jnp.float32)
        * factor
    )
    same_crop = crop_ids[:, None] == crop_ids[None, :]
    return jnp.where(same_crop[None], scores, masked_score)


def attend_forward(factor):

    def attend(pieces):
        query_rows, key_rows, value_rows, crop_ids = pieces
        scores = set_scores(query_rows, key_rows, crop_ids, factor)
        peak_score = jnp.max(scores, axis=-1, keepdims=True)
        raised = jnp.exp(scores - peak_score)
        row_total = jnp.sum(raised, axis=-1, keepdims=True)
        weights = (raised / row_total).astype(jnp.bfloat16)
        mixed = jnp.einsum("hqk,khe->qhe", weights, value_rows, preferred_element_type=jnp.float32)
        return (mixed.astype(jnp.bfloat16), (peak_score + jnp.log(row_total))[..., 0])

    return attend


def attend_backward(factor):

    def backward(pieces):
        query_rows, key_rows, value_rows, crop_ids, log_total, grad_mixed = pieces
        scores = set_scores(query_rows, key_rows, crop_ids, factor)
        weights = jnp.exp(scores - log_total[..., None])
        grad_values = jnp.einsum(
            "hqk,qhe->khe",
            weights.astype(jnp.bfloat16),
            grad_mixed,
            preferred_element_type=jnp.float32,
        )
        grad_weights = jnp.einsum(
            "qhe,khe->hqk", grad_mixed, value_rows, preferred_element_type=jnp.float32
        )
        grad_scores = weights * (
            grad_weights - jnp.sum(weights * grad_weights, axis=-1, keepdims=True)
        )
        scores_low = grad_scores.astype(jnp.bfloat16)
        grad_queries = (
            jnp.einsum("hqk,khe->qhe", scores_low, key_rows, preferred_element_type=jnp.float32)
            * factor
        )
        grad_keys = (
            jnp.einsum("hqk,qhe->khe", scores_low, query_rows, preferred_element_type=jnp.float32)
            * factor
        )
        return (grad_queries, grad_keys, grad_values)

    return backward


def shards(
    tokens,
    offsets,
    first_gain,
    first_shift,
    qkv_weight,
    qv_bias,
    proj_weight,
    proj_bias,
    second_gain,
    second_shift,
    expand_weight,
    expand_bias,
    shrink_weight,
    shrink_bias,
    cotangent,
):
    row_count = tokens.shape[0]
    sets_here = offsets.shape[0]
    width_here = qkv_weight.shape[2]
    local_heads = width_here // HEAD_DIM
    factor = HEAD_DIM ** (-0.5)
    model_count = lax.axis_size("mp")
    model_index = lax.axis_index("mp")
    extra = -row_count % model_count
    share_rows = (row_count + extra) // model_count
    share_start = model_index * share_rows
    row_numbers = jnp.arange(row_count, dtype=jnp.int32)
    row_mask = ((row_numbers >= share_start) & (row_numbers < share_start + share_rows)).astype(
        jnp.float32
    )[:, None]
    positions = jnp.arange(SET_TOKENS, dtype=jnp.int32)
    crop_ids = jnp.sum((positions[None, :, None] >= offsets[:, None, :]).astype(jnp.int32), axis=-1)
    qkv_master = qkv_weight.astype(jnp.bfloat16)
    proj_master = proj_weight.astype(jnp.bfloat16)
    expand_master = expand_weight.astype(jnp.bfloat16)
    shrink_master = shrink_weight.astype(jnp.bfloat16)
    qkv_full, proj_full, expand_full, shrink_full = (
        lax.all_gather(qkv_master, "dp", axis=0, tiled=True),
        lax.all_gather(proj_master, "dp", axis=1, tiled=True),
        lax.all_gather(expand_master, "dp", axis=0, tiled=True),
        lax.all_gather(shrink_master, "dp", axis=1, tiled=True),
    )
    inputs = tokens.astype(jnp.float32)
    first_low = layer_norm(inputs, first_gain, first_shift).astype(jnp.bfloat16)
    projected = jnp.einsum("td,dcf->tcf", first_low, qkv_full, preferred_element_type=jnp.float32)
    shaped = (sets_here, SET_TOKENS, local_heads, HEAD_DIM)
    query_rows = (projected[:, 0] + qv_bias[0]).astype(jnp.bfloat16).reshape(shaped)
    key_rows = projected[:, 1].astype(jnp.bfloat16).reshape(shaped)
    value_rows = (projected[:, 2] + qv_bias[1]).astype(jnp.bfloat16).reshape(shaped)
    attended, log_total = lax.map(
        attend_forward(factor), (query_rows, key_rows, value_rows, crop_ids)
    )
    attended_flat = attended.reshape(row_count, width_here)
    attn_part = matmul(attended_flat, proj_full)
    residual = inputs + lax.psum(attn_part, "mp") + proj_bias
    second_low = layer_norm(residual, second_gain, second_shift).astype(jnp.bfloat16)
    hidden_pre = matmul(second_low, expand_full) + expand_bias
    hidden = gelu(hidden_pre).astype(jnp.bfloat16)
    mlp_part = matmul(hidden, shrink_full)
    outputs = (
        residual + lax.psum(mlp_part.astype(jnp.bfloat16), "mp").astype(jnp.float32) + shrink_bias
    ).astype(jnp.bfloat16)
    grad_out = cotangent.astype(jnp.float32)
    shrink_grad = jnp.einsum("tf,td->fd", hidden, cotangent, preferred_element_type=jnp.float32)
    grad_hidden = jnp.einsum(
        "td,fd->tf", cotangent, shrink_full, preferred_element_type=jnp.float32
    )
    _, gelu_pull = jax.vjp(gelu, hidden_pre)
    grad_pre = gelu_pull(grad_hidden)[0]
    expand_bias_grad = jnp.sum(grad_pre, axis=0)
    grad_pre_low = grad_pre.astype(jnp.bfloat16)
    expand_grad = jnp.einsum(
        "td,tf->df", second_low, grad_pre_low, preferred_element_type=jnp.float32
    )
    second_part = jnp.einsum(
        "tf,df->td", grad_pre_low, expand_full, preferred_element_type=jnp.float32
    )
    grad_second = lax.psum(second_part, "mp")
    _, second_pull = jax.vjp(lambda values: layer_norm(values, second_gain, second_shift), residual)
    grad_residual = second_pull(grad_second)[0] + grad_out
    grad_second_kept = grad_second * row_mask
    second_gain_grad = jnp.sum(grad_second_kept * normalized(residual), axis=0)
    second_shift_grad = jnp.sum(grad_second_kept, axis=0)
    proj_bias_grad = jnp.sum(grad_residual * row_mask, axis=0)
    shrink_bias_grad = jnp.sum(grad_out * row_mask, axis=0)
    residual_low = grad_residual.astype(jnp.bfloat16)
    proj_grad = jnp.einsum(
        "tc,td->cd", attended_flat, residual_low, preferred_element_type=jnp.float32
    )
    grad_attended = jnp.einsum(
        "td,cd->tc", residual_low, proj_full, preferred_element_type=jnp.float32
    ).astype(jnp.bfloat16)
    grad_queries, grad_keys, grad_values = lax.map(
        attend_backward(factor),
        (query_rows, key_rows, value_rows, crop_ids, log_total, grad_attended.reshape(shaped)),
    )
    grad_queries = grad_queries.reshape(row_count, width_here)
    grad_keys = grad_keys.reshape(row_count, width_here)
    grad_values = grad_values.reshape(row_count, width_here)
    qv_bias_grad = jnp.stack([jnp.sum(grad_queries, axis=0), jnp.sum(grad_values, axis=0)])
    grad_projected = jnp.stack([grad_queries, grad_keys, grad_values], axis=1).astype(jnp.bfloat16)
    qkv_grad = jnp.einsum(
        "td,tcf->dcf", first_low, grad_projected, preferred_element_type=jnp.float32
    )
    first_part = jnp.einsum(
        "tcf,dcf->td", grad_projected, qkv_full, preferred_element_type=jnp.float32
    )
    grad_first = lax.psum(first_part.astype(jnp.bfloat16), "mp").astype(jnp.float32)
    _, first_pull = jax.vjp(lambda values: layer_norm(values, first_gain, first_shift), inputs)
    grad_tokens = first_pull(grad_first)[0] + grad_residual
    grad_first_kept = grad_first * row_mask
    first_gain_grad = jnp.sum(grad_first_kept * normalized(inputs), axis=0)
    first_shift_grad = jnp.sum(grad_first_kept, axis=0)
    qkv_part, proj_part, expand_part, shrink_part = (
        lax.psum_scatter(
            qkv_grad.astype(jnp.bfloat16), "dp", scatter_dimension=0, tiled=True
        ).astype(jnp.float32),
        lax.psum_scatter(
            proj_grad.astype(jnp.bfloat16), "dp", scatter_dimension=1, tiled=True
        ).astype(jnp.float32),
        lax.psum_scatter(
            expand_grad.astype(jnp.bfloat16), "dp", scatter_dimension=0, tiled=True
        ).astype(jnp.float32),
        lax.psum_scatter(
            shrink_grad.astype(jnp.bfloat16), "dp", scatter_dimension=1, tiled=True
        ).astype(jnp.float32),
    )
    qv_part, expand_bias_part = lax.psum((qv_bias_grad, expand_bias_grad), "dp")
    small_parts = lax.psum(
        (
            first_gain_grad,
            first_shift_grad,
            proj_bias_grad,
            second_gain_grad,
            second_shift_grad,
            shrink_bias_grad,
        ),
        ("dp", "mp"),
    )
    return (
        outputs,
        grad_tokens,
        small_parts[0],
        small_parts[1],
        qkv_part,
        qv_part,
        proj_part,
        small_parts[2],
        small_parts[3],
        small_parts[4],
        expand_part,
        expand_bias_part,
        shrink_part,
        small_parts[5],
    )


def solution(mesh):
    placed = (
        P("dp", None),
        P("dp", None),
        P(),
        P(),
        P("dp", None, "mp"),
        P(None, "mp"),
        P("mp", "dp"),
        P(),
        P(),
        P(),
        P("dp", "mp"),
        P("mp"),
        P("mp", "dp"),
        P(),
        P("dp", None),
    )
    return jax.shard_map(
        shards,
        mesh=mesh,
        in_specs=placed,
        out_specs=(
            P("dp", None),
            P("dp", None),
            P(),
            P(),
            P("dp", None, "mp"),
            P(None, "mp"),
            P("mp", "dp"),
            P(),
            P(),
            P(),
            P("dp", "mp"),
            P("mp"),
            P("mp", "dp"),
            P(),
        ),
        check_vma=False,
    )
```

profile of v0, /device:TPU:0, one launch (start us, length us, event | category | flops | bytes accessed | tf_op | source)
XLA Modules:
  0.0 1080.6 jit_solution(10375636445222786847)
XLA Ops:
  16.9 34.5 %all_gather.13 = bf16[256,1024]{1,0:T(8,128)(2,1)} all-gather(bf16[256,128]{1,0:T(8,128)(2,1)S(1)} %convert_element_type.121), channel_id=1, replica_groups=mesh['dp'=8,'mp'=4] {'dp'}, dimensions={1}, use_global_device_ids=true | all-gather | bytes 589824 | tf_op jit(solution)/shard_map/all_gather | solution.py:130
  51.4 10.1 all-gather.4.cloned.1.call-done
  94.1 20.2 %while.26 = (s32[]{:T(128)}, bf16[6,345,4,64]{1,3,2,0:T(8,128)(2,1)}, f32[6,4,345]{2,1,0:T(4,128)}, bf16[6,345,4,64]{1,3,2,0:T(8,128)(2,1)S(1)}, s32[6,345]{1,0:...) while((s32[]{:T(128)}, ...), condition=%wide.region_6.7_spmd, body=%wide.region_3.6_spmd.sunk | while | flops 127800768 | bytes 7318627 | solution.py:141
  130.2 151.0 %all-reduce.7.cloned.1.call-done = f32[2070,1024]{1,0:T(8,128)} async-done(((f32[2070,1024]{1,0:T(8,128)}), f32[2070,1024]{1,0:T(8,128)}) %all-reduce.7.cloned.1.call-update) | async-done | bytes 8478736 | tf_op jit(solution)/shard_map/psum | solution.py:146
  293.3 40.2 %all-gather.6.cloned.1.call-done = bf16[1024,1024]{1,0:T(8,128)(2,1)} async-done(((bf16[128,1024]{1,0:T(8,128)(2,1)}), bf16[1024,1024]{1,0:T(8,128)(2,1)}) %all-gather.6.cloned.1.call-update) | async-done | bytes 2097168 | tf_op jit(solution)/shard_map/all_gather | solution.py:131
  333.5 10.9 %fusion.88 = f32[2070,1024]{1,0:T(8,128)} fusion(bf16[2070,1024]{1,0:T(8,128)(2,1)} %add_convert_fusion.1, bf16[1024,1024]{1,0:T(8,128)(2,1)} %all-gather.6.cloned.1.call-done), kind=kOutput, calls=%fused_computation.143 | convolution fusion | flops 4341104640 | bytes 14815232 | tf_op jit(solution)/shard_map/dot_general | solution.py:32
  344.4 41.4 %all-gather.8.cloned.1.call-done = bf16[1024,1024]{1,0:T(8,128)(2,1)} async-done(((bf16[1024,128]{1,0:T(8,128)(2,1)}), bf16[1024,1024]{1,0:T(8,128)(2,1)}) %all-gather.8.cloned.1.call-update) | async-done | bytes 2097168 | tf_op jit(solution)/shard_map/all_gather | solution.py:132
  385.8 13.9 %fusion.80 = (f32[1024]{0:T(1024)}, bf16[2070,1024]{1,0:T(8,128)(2,1)S(1)}, bf16[2070,1024]{1,0:T(8,128)(2,1)}) fusion(f32[2070,1024]{1,0:T(8,128)} %fusion.88, f32[1024]{0:T(1024)S(1)} %copy-done.29, bf16[2070,1024]{1,0:T(8,128)(2,1)} %param.33, bf16[1024,1024]{1,0:T(8,128)(2,1)} %all-gather.8.cloned.1.call-done), kind=kOutput, calls=%fused_computation.136 | convolution fusion | flops 4377138176 | bytes 23302144 | tf_op jit(solution)/shard_map/td,fd->tf/dot_general | solution.py:156
  401.7 7.2 fusion.65
  408.9 9.5 convolution_convert_fusion.3
  422.5 9.2 fusion.67
  431.7 130.3 %all-reduce.9.cloned.1.call-done = f32[2070,1024]{1,0:T(8,128)} async-done(((f32[2070,1024]{1,0:T(8,128)}), f32[2070,1024]{1,0:T(8,128)}) %all-reduce.9.cloned.1.call-update) | async-done | bytes 8478736 | tf_op jit(solution)/shard_map/psum | solution.py:169
  562.0 8.2 multiply_reduce_fusion.1
  587.3 46.0 %while.27 = (s32[]{:T(128)}, f32[6,345,4,64]{1,3,2,0:T(8,128)}, bf16[6,345,4,64]{1,3,2,0:T(8,128)(2,1)}, f32[6,345,4,64]{1,3,2,0:T(8,128)}, bf16[6,345,4,64]{1,3...) while((s32[]{:T(128)}, f32[6,345,4,64]{1,3,2,0:T(8,128)}, ...), condition=%wide.region_16.17_spmd, body=%wide.region_14.16_spmd.sunk | while | flops 309283200 | bytes 17905568 | solution.py:184
  668.8 9.3 convolution_convert_fusion.4
  678.3 9.7 convolution_convert_fusion.1
  695.0 8.4 reduce-scatter.11.cloned.1.call-done
  705.5 20.3 %all-reduce.1 = (f32[2,256]{1,0:T(2,128)}, f32[1024]{0:T(1024)}) all-reduce(f32[2,256]{1,0:T(2,128)S(1)} %pad_maximum_fusion, f32[1024]{0:T(1024)S(1)} %copy-done.25), channel_id=1, replica_groups=mesh['dp'=8,'mp'=4] {'dp'}, use_global_device_ids=true, to_apply=%region_27.28 | all-reduce | flops 1536 | bytes 12288 | tf_op jit(solution)/shard_map/psum | solution.py:219
  725.7 42.0 %reduce-scatter.13.cloned.1.call-done = bf16[128,256]{1,0:T(8,128)(2,1)} async-done(((bf16[1024,256]{1,0:T(8,128)(2,1)}), bf16[128,256]{1,0:T(8,128)(2,1)}) %reduce-scatter.13.cloned.1.call-update) | async-done | bytes 65552
  769.4 66.7 %reduce-scatter.9.cloned.1.call-done = bf16[128,3,256]{2,0,1:T(8,128)(2,1)} async-done(((bf16[1024,3,256]{2,0,1:T(8,128)(2,1)}), bf16[128,3,256]{2,0,1:T(8,128)(2,1)}) %reduce-scatter.9.cloned.1.call-update) | async-done | bytes 196624 | tf_op jit(solution)/shard_map/reduce_scatter | solution.py:206
  837.8 155.5 %all-reduce.11.cloned.1.call-done = (bf16[2070,1024]{1,0:T(8,128)(2,1)}, bf16[2070,1024]{1,0:T(8,128)(2,1)}) async-done(((bf16[2070,1024]{1,0:T(8,128)(2,1)}, bf16[2070,1024]{1,0:T(8,128)(2,1)}), (bf16[2070,1024]{1,0:T(8,128)(2,1)}, bf16[2070,1024]{1,0:T(8,128)(2,1)})) %all-reduce.11.cloned.1.call-update) | async-done | bytes 8478736 | tf_op jit(solution)/shard_map/psum | solution.py:152
  998.8 13.9 %fusion.54 = (f32[1024]{0:T(1024)S(1)}, f32[1024]{0:T(1024)S(1)}, f32[1024]{0:T(1024)S(1)}, f32[2070]{0:T(1024)S(1)}, f32[1024]{0:T(1024)S(1)}) fusion(bf16[2070,1024]{1,0:T(8,128)(2,1)} %param.33, f32[2070]{0:T(1024)S(1)} %copy-done.15, f32[2070,1024]{1,0:T(8,128)} %copy-done.2, f32[2070]{0:T(1024)S(1)} %negate_multiply_fusion.1, ...), kind=kLoop, calls=%fused_computation.79 | loop fusion | flops 44507112 | bytes 21266960 | tf_op jit(solution)/shard_map/reduce_sum | solution.py:176
  1012.7 13.7 %add_add_fusion.2 = f32[2070,1024]{1,0:T(8,128)} fusion(bf16[2070,1024]{1,0:T(8,128)(2,1)} %param.19, bf16[2070,1024]{1,0:T(8,128)(2,1)} %get-tuple-element.235, f32[2070]{0:T(1024)S(1)} %negate_multiply_fusion, f32[2070]{0:T(1024)S(1)} %multiply_multiply_fusion, f32[1024]{0:T(1024)S(1)} %copy-done.21, f32[2070]{0:T(1024)S(1)} %copy-done.13, ...), kind=kLoop, calls=%fused_computation.86 | loop fusion | flops 27555840 | bytes 29721016 | tf_op jit(solution)/shard_map/add | solution.py:201
  1033.5 40.0 %all-reduce = (f32[1024]{0:T(1024)}, f32[1024]{0:T(1024)}, f32[1024]{0:T(1024)}, f32[1024]{0:T(1024)}, f32[1024]{0:T(1024)}, /*index=5*/f32[1024]{0:T(1024)}) all-reduce(f32[1024]{0:T(1024)S(1)} %get-tuple-element.189, f32[1024]{0:T(1024)S(1)} %get-tuple-element.187, ...), channel_id=1, replica_groups=mesh['dp'=8,'mp'=4] {'dp','mp'}, use_global_device_ids=true, to_apply=%region_21.22 | all-reduce | flops 6144 | bytes 49152 | tf_op jit(solution)/shard_map/psum | solution.py:220
  (260 shorter events, 219.5 us)
Async XLA Ops:
  7.2 54.3 %all-gather.4.cloned.1.call-start = ((), (), s32[]{:S(2)}) async-start(), calls=%async_computation.4 | async-start | bytes 1769472 | tf_op jit(solution)/shard_map/all_gather | solution.py:129
  8.9 272.3 %all-reduce.7.cloned.1.call-start = ((), (), s32[]{:S(2)}) async-start(), calls=%async_computation.5 | async-start | bytes 16973824 | tf_op jit(solution)/shard_map/psum | solution.py:146
  11.9 49.6 %copy-start.20 = (f32[1024]{0:T(1024)S(1)}, f32[1024]{0:T(1024)}, u32[]{:S(2)}) copy-start(f32[1024]{0:T(1024)} %param.21) | copy-start | bytes 12292
  11.9 49.6 %copy-start.30 = (f32[1024]{0:T(1024)S(1)}, f32[1024]{0:T(1024)}, u32[]{:S(2)}) copy-start(f32[1024]{0:T(1024)} %param.22) | copy-start | bytes 12292
  15.0 53.0 %copy-start.10 = (f32[2070]{0:T(1024)}, f32[2070]{0:T(1024)S(1)}, u32[]{:S(2)}) copy-start(f32[2070]{0:T(1024)S(1)} %broadcast_multiply_fusion.1) | copy-start | bytes 24844
  16.9 51.1 %copy-start.12 = (f32[2070]{0:T(1024)}, f32[2070]{0:T(1024)S(1)}, u32[]{:S(2)}) copy-start(f32[2070]{0:T(1024)S(1)} %fusion.78) | copy-start | bytes 24844
  114.3 13.1 %copy-start.18 = (s32[6,345]{1,0:T(8,128)}, s32[6,345]{1,0:T(8,128)S(1)}, u32[]{:S(2)}) copy-start(s32[6,345]{1,0:T(8,128)S(1)} %get-tuple-element.473) | copy-start | bytes 24844
  127.4 153.9 %copy-start.26 = (f32[1024]{0:T(1024)S(1)}, f32[1024]{0:T(1024)}, u32[]{:S(2)}) copy-start(f32[1024]{0:T(1024)} %param.26) | copy-start | bytes 12292
  127.4 206.1 %all-gather.6.cloned.1.call-start = ((), (), s32[]{:S(2)}) async-start(), calls=%async_computation.6 | async-start | bytes 2359296 | tf_op jit(solution)/shard_map/all_gather | solution.py:131
  129.2 256.6 %all-gather.8.cloned.1.call-start = ((), (), s32[]{:S(2)}) async-start(), calls=%async_computation.7 | async-start | bytes 2359296 | tf_op jit(solution)/shard_map/all_gather | solution.py:132
  130.0 432.0 %all-reduce.9.cloned.1.call-start = ((), (), s32[]{:S(2)}) async-start(), calls=%async_computation.8 | async-start | bytes 16973824 | tf_op jit(solution)/shard_map/psum | solution.py:169
  293.3 92.5 %copy-start.29 = (f32[1024]{0:T(1024)S(1)}, f32[1024]{0:T(1024)}, u32[]{:S(2)}) copy-start(f32[1024]{0:T(1024)} %param.30) | copy-start | bytes 12292
  385.8 15.9 %copy-start.27 = (bf16[1024,1024]{1,0:T(8,128)(2,1)S(1)}, bf16[1024,1024]{1,0:T(8,128)(2,1)}, u32[]{:S(2)}) copy-start(bf16[1024,1024]{1,0:T(8,128)(2,1)} %all-gather.6.cloned.1.call-done) | copy-start | bytes 6291460
  408.8 284.2 %reduce-scatter.15.cloned.1.call-start = ((), (), s32[]{:S(2)}) async-start(), calls=%async_computation.12 | async-start | bytes 2359296
  422.4 281.1 %reduce-scatter.11.cloned.1.call-start = ((), (), s32[]{:S(2)}) async-start(), calls=%async_computation.10 | async-start | bytes 2359296 | tf_op jit(solution)/shard_map/reduce_scatter | solution.py:212
  422.5 139.5 %copy-start.14 = (f32[2070]{0:T(1024)}, f32[2070]{0:T(1024)S(1)}, u32[]{:S(2)}) copy-start(f32[2070]{0:T(1024)S(1)} %fusion.77) | copy-start | bytes 24844
  431.7 336.1 %reduce-scatter.13.cloned.1.call-start = ((), (), s32[]{:S(2)}) async-start(), calls=%async_computation.11 | async-start | bytes 589824
  562.0 17.4 %slice-start = ((s8[4243456]{0:T(1024)(128)(4,1)}), s8[4194304]{0:T(1024)(128)(4,1)S(1)}, s32[]{:S(2)}) async-start(s8[4243456]{0:T(1024)(128)(4,1)} %bitcast.139), calls=%async_computation.14 | async-start | bytes 8388608
  665.4 170.7 %reduce-scatter.9.cloned.1.call-start = ((), (), s32[]{:S(2)}) async-start(), calls=%async_computation.9 | async-start | bytes 1769472 | tf_op jit(solution)/shard_map/reduce_scatter | solution.py:206
  678.2 315.1 %all-reduce.11.cloned.1.call-start = ((), (), s32[]{:S(2)}) async-start(), calls=%async_computation.13 | async-start | bytes 16973824 | tf_op jit(solution)/shard_map/psum | solution.py:152
  693.0 12.4 %copy-start.25 = (f32[1024]{0:T(1024)S(1)}, f32[1024]{0:T(1024)}, u32[]{:S(2)}) copy-start(f32[1024]{0:T(1024)} %get-tuple-element.236) | copy-start | bytes 12292
  998.8 27.6 %slice-start.2 = ((s8[4243456]{0:T(1024)(128)(4,1)}), s8[49152]{0:T(1024)(128)(4,1)S(1)}, s32[]{:S(2)}) async-start(s8[4243456]{0:T(1024)(128)(4,1)} %bitcast.142), calls=%async_computation.16 | async-start | bytes 98304
  1012.7 13.7 %slice-start.3 = ((s8[4243456]{0:T(1024)(128)(4,1)}), s8[4194304]{0:T(1024)(128)(4,1)S(1)}, s32[]{:S(2)}) async-start(s8[4243456]{0:T(1024)(128)(4,1)} %bitcast.142), calls=%async_computation.17 | async-start | bytes 8388608
  1012.7 13.7 %copy-start.24 = (f32[1024]{0:T(1024)S(1)}, f32[1024]{0:T(1024)}, u32[]{:S(2)}) copy-start(f32[1024]{0:T(1024)} %param.32) | copy-start | bytes 12292
  (23 other events, 127.0 us)
Sparse Core Ops, SparseCore 0:
  10.8 50.6 all-gather.3
  127.6 153.6 all-reduce.6
  284.2 49.2 all-gather.5
  336.2 49.5 all-gather.7
  409.0 152.9 all-reduce.8
  565.4 67.6 reduce-scatter.14
  636.6 66.8 reduce-scatter.10
  706.8 60.8 reduce-scatter.12
  771.6 64.4 reduce-scatter.8
  839.1 154.1 all-reduce.10
where the time goes:
time: 1080 us
  waiting for transfers between devices  646 us (60%)
  matrix products  143 us (13%)
  other arithmetic  95.7 us (9%)
  blocking collectives  94.8 us (9%)
  local copies, waits for them, and re-layouts  85.2 us (8%)
  between operations  15 us (1%)
    psum x1, waiting for transfers between devices, shards(): lax.psum(mlp_part.astype(jnp.bfloat16), 'mp').astype(jnp.float32)  156 us
    psum x1, waiting for transfers between devices, shards(): residual = inputs + lax.psum(attn_part, 'mp') + proj_bias  151 us
    psum x1, waiting for transfers between devices, shards(): grad_second = lax.psum(second_part, 'mp')  130 us
    reduce_scatter x1, waiting for transfers between devices, shards(): lax.psum_scatter(qkv_grad.astype(jnp.bfloat16), 'dp', scatter_dimension=0...  66.7 us
    unnamed x12, waiting for transfers between devices  42.2 us
    all_gather x1, waiting for transfers between devices, shards(): lax.all_gather(shrink_master, 'dp', axis=1, tiled=True)  41.4 us
    all_gather x1, waiting for transfers between devices, shards(): lax.all_gather(expand_master, 'dp', axis=0, tiled=True)  40.2 us
    psum x1, blocking collectives, shards(): lax.psum((first_gain_grad, first_shift_grad, proj_bias_grad, second_gain_...  40 us
  transfers between devices with their start and end apart: 10, of which 9 were waited for; matrix products, arithmetic and copies ran while one was open for 17% of the time, Pallas kernels for 0%

commit v1 on v0

--- a/solution.py
+++ b/solution.py
@@ -8,6 +8,28 @@
 norm_eps = 1e-06
 masked_score = -1e30
 root_half = 0.7071067811865476
+
+
+def laid_out(blocks, dim):
+    blocks = jnp.moveaxis(blocks, 0, dim)
+    shape = blocks.shape
+    return blocks.reshape(*shape[:dim], shape[dim] * shape[dim + 1], *shape[dim + 2 :])
+
+
+def collect(x, axis, dim):
+    size = lax.axis_size(axis)
+    pairs = [(i, (i + 1) % size) for i in range(size)]
+    back = [(b, a) for a, b in pairs]
+    lower, upper = ([], [])
+    for lap in range(size - 1):
+        if lap % 2 == 0:
+            lower.append(lax.ppermute(lower[-1] if lower else x, axis, pairs))
+        else:
+            upper.append(lax.ppermute(upper[-1] if upper else x, axis, back))
+    blocks = jnp.stack([*lower[::-1], x, *upper])
+    shift = lax.axis_index(axis) - len(lower)
+    blocks = blocks[(jnp.arange(size) - shift) % size]
+    return laid_out(blocks, dim)
 
 
 def layer_norm(values, gain, shift):
@@ -128,7 +150,7 @@
     qkv_full, proj_full, expand_full, shrink_full = (
         lax.all_gather(qkv_master, "dp", axis=0, tiled=True),
         lax.all_gather(proj_master, "dp", axis=1, tiled=True),
-        lax.all_gather(expand_master, "dp", axis=0, tiled=True),
+        collect(expand_master, "dp", 0),
         lax.all_gather(shrink_master, "dp", axis=1, tiled=True),
     )
     inputs = tokens.astype(jnp.float32)

time: 1080 us -> 990 us (0.917)
  waiting for transfers between devices: 646 us -> 527 us
  starting transfers between devices: 0.59 us -> 16 us
    psum x1, waiting for transfers between devices: 151 us -> 84.5 us  [shards(): residual = inputs + lax.psum(attn_part, 'mp') + proj_bias]
    all_gather x1, waiting for transfers between devices: 41.4 us -> 0.01 us  [shards(): lax.all_gather(shrink_master, 'dp', axis=1, tiled=True)]
    all_gather x1 -> x0, waiting for transfers between devices: 40.2 us -> none  [shards(): lax.all_gather(expand_master, 'dp', axis=0, tiled=True)]
    ppermute x0 -> x7, waiting for transfers between devices: none -> 29.5 us  [the longest x4 29.5 us: collect(): lower.append(lax.ppermute(lower[-1] if lower else x, axis, pairs))]
    ppermute x0 -> x7, starting transfers between devices: none -> 15 us  [the longest x3 9.32 us: collect(): upper.append(lax.ppermute(upper[-1] if upper else x, axis, back))]
    unnamed x81 -> x97, local copies, waits for them, and re-layouts: 22.8 us -> 28.9 us
    unnamed x12 -> x11, waiting for transfers between devices: 42.2 us -> 42.2 us
  transfers between devices with their start and end apart: 10 -> 16, of which waited for: 9 -> 11; matrix products, arithmetic and copies ran while one was open for 17% -> 26% of each run, Pallas kernels for 0% -> 0%
where the time goes in v1:
time: 990 us; the launch traced here: 985 us
  waiting for transfers between devices  527 us (53%)
  matrix products  147 us (15%)
  local copies, waits for them, and re-layouts  94.8 us (10%)
  blocking collectives  93.7 us (9%)
  other arithmetic  91.1 us (9%)
  starting transfers between devices  16 us (2%)
  between operations  14.8 us (1%)
    psum x1, waiting for transfers between devices, shards(): lax.psum(mlp_part.astype(jnp.bfloat16), 'mp').astype(jnp.float32)  156 us
    psum x1, waiting for transfers between devices, shards(): grad_second = lax.psum(second_part, 'mp')  129 us
    psum x1, waiting for transfers between devices, shards(): residual = inputs + lax.psum(attn_part, 'mp') + proj_bias  84.5 us
    reduce_scatter x1, waiting for transfers between devices, shards(): lax.psum_scatter(qkv_grad.astype(jnp.bfloat16), 'dp', scatter_dimension=0...  66.7 us
    unnamed x11, waiting for transfers between devices  42.2 us
    psum x1, blocking collectives, shards(): lax.psum((first_gain_grad, first_shift_grad, proj_bias_grad, second_gain_...  39.9 us
    all_gather x1, blocking collectives, shards(): lax.all_gather(proj_master, 'dp', axis=1, tiled=True)  33.5 us
    dot_general x3, matrix products, matmul(): return jnp.dot(left, right, preferred_element_type=jnp.float32)  30.1 us
  transfers between devices with their start and end apart: 16, of which 11 were waited for; matrix products, arithmetic and copies ran while one was open for 26% of the time, Pallas kernels for 0%

profile of v1, /device:TPU:0, one launch (start us, length us, event | category | flops | bytes accessed | tf_op | source)
XLA Modules:
  0.0 985.0 jit_solution(11312355912221909215)
XLA Ops:
  16.6 33.5 %all_gather.10 = bf16[256,1024]{1,0:T(8,128)(2,1)} all-gather(bf16[256,128]{1,0:T(8,128)(2,1)S(1)} %convert_element_type.121), channel_id=1, replica_groups=mesh['dp'=8,'mp'=4] {'dp'}, dimensions={1}, use_global_device_ids=true | all-gather | bytes 589824 | tf_op jit(solution)/shard_map/all_gather | solution.py:152
  50.2 10.6 %all-gather.3.cloned.1.call-done = bf16[1024,3,256]{2,0,1:T(8,128)(2,1)} async-done(((bf16[128,3,256]{2,0,1:T(8,128)(2,1)}), bf16[1024,3,256]{2,0,1:T(8,128)(2,1)}) %all-gather.3.cloned.1.call-update) | async-done | bytes 1572880 | tf_op jit(solution)/shard_map/all_gather | solution.py:151
  91.7 21.8 %while.26 = (s32[]{:T(128)}, bf16[6,345,4,64]{1,3,2,0:T(8,128)(2,1)S(1)}, f32[6,4,345]{2,1,0:T(4,128)}, bf16[6,345,4,64]{1,3,2,0:T(8,128)(2,1)}, s32[6,345]{1,0:...) while((s32[]{:T(128)}, ...), condition=%wide.region_6.7_spmd, body=%wide.region_3.6_spmd.sunk | while | flops 127800768 | bytes 7319127 | solution.py:163
  126.0 9.5 collective-permute-done
  150.2 7.5 collective-permute-done.2
  162.7 7.3 collective-permute-done.3
  183.2 10.9 %fusion.90 = f32[2070,1024]{1,0:T(8,128)} fusion(bf16[2070,1024]{1,0:T(8,128)(2,1)} %param.33, bf16[1024,1024]{1,0:T(8,128)(2,1)} %all-gather.5.cloned.1.call-done), kind=kOutput, calls=%fused_computation.159 | convolution fusion | flops 4341104640 | bytes 14815232 | tf_op jit(solution)/shard_map/td,fd->tf/dot_general | solution.py:178
  194.0 84.5 %all-reduce.7.cloned.1.call-done = f32[2070,1024]{1,0:T(8,128)} async-done(((f32[2070,1024]{1,0:T(8,128)}), f32[2070,1024]{1,0:T(8,128)}) %all-reduce.7.cloned.1.call-update) | async-done | bytes 8478736 | tf_op jit(solution)/shard_map/psum | solution.py:168
  288.0 14.3 %fusion.82 = (f32[1024]{0:T(1024)}, bf16[2070,1024]{1,0:T(8,128)(2,1)S(1)}, bf16[2070,1024]{1,0:T(8,128)(2,1)}) fusion(f32[2070,1024]{1,0:T(8,128)} %fusion.90, f32[1024]{0:T(1024)S(1)} %copy-done.33, bf16[1024,1024]{1,0:T(8,128)(2,1)S(1)} %bitcast.161, f32[2070,1024]{1,0:T(8,128)S(1)} %get-tuple-element.241, f32[1024]{0:T(1024)S(1)} %copy-done.34, ...), kind=kOutput, calls=%fused_computation.152 | convolution fusion | flops 4387736576 | bytes 27566256 | tf_op jit(solution)/shard_map/dot_general | solution.py:54
  311.7 9.2 convolution_convert_fusion.3
  325.0 12.1 %fusion.67 = bf16[1024,1024]{1,0:T(8,128)(2,1)} fusion(bf16[2070,1024]{1,0:T(8,128)(2,1)} %copy-done.37, f32[2070,1024]{1,0:T(8,128)} %copy-done, f32[1024]{0:T(1024)S(1)} %copy-done.34, f32[1024]{0:T(1024)S(1)} %copy-done.25, f32[2070]{0:T(1024)S(1)} %fusion.79, f32[2070]{0:T(1024)S(1)} %broadcast_multiply_fusion), kind=kOutput, calls=%fused_computation.111 | convolution fusion | flops 4352751616 | bytes 14839984 | tf_op jit(solution)/shard_map/td,tf->df/dot_general | solution.py:185
  337.6 128.8 %all-reduce.9.cloned.1.call-done = f32[2070,1024]{1,0:T(8,128)} async-done(((f32[2070,1024]{1,0:T(8,128)}), f32[2070,1024]{1,0:T(8,128)}) %all-reduce.9.cloned.1.call-update) | async-done | bytes 8478736 | tf_op jit(solution)/shard_map/psum | solution.py:191
  466.4 8.2 multiply_reduce_fusion.1
  491.8 45.9 %while.27 = (s32[]{:T(128)}, f32[6,345,4,64]{1,3,2,0:T(8,128)}, bf16[6,345,4,64]{1,3,2,0:T(8,128)(2,1)}, f32[6,345,4,64]{1,3,2,0:T(8,128)}, bf16[6,345,4,64]{1,3...) while((s32[]{:T(128)}, f32[6,345,4,64]{1,3,2,0:T(8,128)}, ...), condition=%wide.region_16.17_spmd, body=%wide.region_14.16_spmd.sunk | while | flops 309283200 | bytes 17905560 | solution.py:206
  573.2 9.4 convolution_convert_fusion.4
  582.6 9.6 convolution_convert_fusion.1
  599.3 8.7 reduce-scatter.11.cloned.1.call-done
  610.0 20.2 %all-reduce.1 = (f32[2,256]{1,0:T(2,128)}, f32[1024]{0:T(1024)}) all-reduce(f32[2,256]{1,0:T(2,128)S(1)} %pad_maximum_fusion, f32[1024]{0:T(1024)S(1)} %copy-done.28), channel_id=1, replica_groups=mesh['dp'=8,'mp'=4] {'dp'}, use_global_device_ids=true, to_apply=%region_27.28 | all-reduce | flops 1536 | bytes 12288 | tf_op jit(solution)/shard_map/psum | solution.py:241
  630.2 42.0 %reduce-scatter.13.cloned.1.call-done = bf16[128,256]{1,0:T(8,128)(2,1)} async-done(((bf16[1024,256]{1,0:T(8,128)(2,1)}), bf16[128,256]{1,0:T(8,128)(2,1)}) %reduce-scatter.13.cloned.1.call-update) | async-done | bytes 65552
  673.9 66.7 %reduce-scatter.9.cloned.1.call-done = bf16[128,3,256]{2,0,1:T(8,128)(2,1)} async-done(((bf16[1024,3,256]{2,0,1:T(8,128)(2,1)}), bf16[128,3,256]{2,0,1:T(8,128)(2,1)}) %reduce-scatter.9.cloned.1.call-update) | async-done | bytes 196624 | tf_op jit(solution)/shard_map/reduce_scatter | solution.py:228
  742.3 155.7 %all-reduce.11.cloned.1.call-done = (bf16[2070,1024]{1,0:T(8,128)(2,1)}, bf16[2070,1024]{1,0:T(8,128)(2,1)}) async-done(((bf16[2070,1024]{1,0:T(8,128)(2,1)}, bf16[2070,1024]{1,0:T(8,128)(2,1)}), (bf16[2070,1024]{1,0:T(8,128)(2,1)}, bf16[2070,1024]{1,0:T(8,128)(2,1)})) %all-reduce.11.cloned.1.call-update) | async-done | bytes 8478736 | tf_op jit(solution)/shard_map/psum | solution.py:174
  903.4 14.0 %fusion.54 = (f32[1024]{0:T(1024)S(1)}, f32[1024]{0:T(1024)S(1)}, f32[1024]{0:T(1024)S(1)}, f32[2070]{0:T(1024)S(1)}, f32[1024]{0:T(1024)S(1)}) fusion(bf16[2070,1024]{1,0:T(8,128)(2,1)} %param.33, f32[2070]{0:T(1024)S(1)} %copy-done.19, f32[2070,1024]{1,0:T(8,128)} %copy-done.2, f32[2070]{0:T(1024)S(1)} %negate_multiply_fusion.1, ...), kind=kLoop, calls=%fused_computation.80 | loop fusion | flops 44507112 | bytes 21266960 | tf_op jit(solution)/shard_map/reduce_sum | solution.py:198
  917.4 13.7 %add_add_fusion.2 = f32[2070,1024]{1,0:T(8,128)} fusion(bf16[2070,1024]{1,0:T(8,128)(2,1)} %param.19, bf16[2070,1024]{1,0:T(8,128)(2,1)} %get-tuple-element.235, f32[2070]{0:T(1024)S(1)} %negate_multiply_fusion, f32[2070]{0:T(1024)S(1)} %multiply_multiply_fusion, f32[1024]{0:T(1024)S(1)} %copy-done.24, f32[2070]{0:T(1024)S(1)} %copy-done.17, ...), kind=kLoop, calls=%fused_computation.87 | loop fusion | flops 27555840 | bytes 29721016 | tf_op jit(solution)/shard_map/add | solution.py:223
  938.3 39.9 %all-reduce = (f32[1024]{0:T(1024)}, f32[1024]{0:T(1024)}, f32[1024]{0:T(1024)}, f32[1024]{0:T(1024)}, f32[1024]{0:T(1024)}, /*index=5*/f32[1024]{0:T(1024)}) all-reduce(f32[1024]{0:T(1024)S(1)} %get-tuple-element.189, f32[1024]{0:T(1024)S(1)} %get-tuple-element.187, ...), channel_id=1, replica_groups=mesh['dp'=8,'mp'=4] {'dp','mp'}, use_global_device_ids=true, to_apply=%region_21.22 | all-reduce | flops 6144 | bytes 49152 | tf_op jit(solution)/shard_map/psum | solution.py:242
  (291 shorter events, 253.4 us)
Async XLA Ops:
  7.2 53.6 %all-gather.3.cloned.1.call-start = ((), (), s32[]{:S(2)}) async-start(), calls=%async_computation.4 | async-start | bytes 1769472 | tf_op jit(solution)/shard_map/all_gather | solution.py:151
  8.9 174.2 %all-gather.5.cloned.1.call-start = ((), (), s32[]{:S(2)}) async-start(), calls=%async_computation.6 | async-start | bytes 2359296 | tf_op jit(solution)/shard_map/all_gather | solution.py:154
  10.8 267.8 %all-reduce.7.cloned.1.call-start = ((), (), s32[]{:S(2)}) async-start(), calls=%async_computation.5 | async-start | bytes 16973824 | tf_op jit(solution)/shard_map/psum | solution.py:168
  10.9 49.9 %copy-start.23 = (f32[1024]{0:T(1024)S(1)}, f32[1024]{0:T(1024)}, u32[]{:S(2)}) copy-start(f32[1024]{0:T(1024)} %param.21) | copy-start | bytes 12292
  10.9 49.9 %copy-start.35 = (f32[1024]{0:T(1024)S(1)}, f32[1024]{0:T(1024)}, u32[]{:S(2)}) copy-start(f32[1024]{0:T(1024)} %param.22) | copy-start | bytes 12292
  14.3 46.4 %copy-start.12 = (f32[2070]{0:T(1024)}, f32[2070]{0:T(1024)S(1)}, u32[]{:S(2)}) copy-start(f32[2070]{0:T(1024)S(1)} %broadcast_multiply_fusion.1) | copy-start | bytes 24844
  16.2 44.5 %copy-start.16 = (f32[2070]{0:T(1024)}, f32[2070]{0:T(1024)S(1)}, u32[]{:S(2)}) copy-start(f32[2070]{0:T(1024)S(1)} %fusion.78) | copy-start | bytes 24844
  124.3 342.1 %all-reduce.9.cloned.1.call-start = ((), (), s32[]{:S(2)}) async-start(), calls=%async_computation.7 | async-start | bytes 16973824 | tf_op jit(solution)/shard_map/psum | solution.py:191
  125.4 10.2 %collective-permute-start = (bf16[128,1024]{1,0:T(8,128)(2,1)S(1)}, bf16[128,1024]{1,0:T(8,128)(2,1)S(1)}, u32[]{:S(2)}, u32[]{:S(2)}) collective-permute-start(bf16[128,1024]{1,0:T(8,128)(2,1)S(1)} %convert_element_type.123), channel_id=1, source_target_pairs={{0,4},{4,8},{8,12},{12,16},{16,20},{20,24},{24,28},{28,0},{1,5},{5... | collective-permute-start | bytes 786440 | tf_op jit(solution)/shard_map/ppermute | solution.py:26
  135.6 9.9 %collective-permute-start.1 = (bf16[128,1024]{1,0:T(8,128)(2,1)S(1)}, bf16[128,1024]{1,0:T(8,128)(2,1)S(1)}, u32[]{:S(2)}, u32[]{:S(2)}) collective-permute-start(bf16[128,1024]{1,0:T(8,128)(2,1)S(1)} %collective-permute-done), channel_id=1, source_target_pairs={{0,4},{4,8},{8,12},{12,16},{16,20},{20,24},{24,28},{28,0},{1,5},{5... | collective-permute-start | bytes 786440 | tf_op jit(solution)/shard_map/ppermute | solution.py:26
  135.6 12.4 %collective-permute-start.4 = (bf16[128,1024]{1,0:T(8,128)(2,1)S(1)}, bf16[128,1024]{1,0:T(8,128)(2,1)S(1)}, u32[]{:S(2)}, u32[]{:S(2)}) collective-permute-start(bf16[128,1024]{1,0:T(8,128)(2,1)S(1)} %convert_element_type.123), channel_id=1, source_target_pairs={{4,0},{8,4},{12,8},{16,12},{20,16},{24,20},{28,24},{0,28},{5,1},{9... | collective-permute-start | bytes 786440 | tf_op jit(solution)/shard_map/ppermute | solution.py:28
  145.5 12.2 %collective-permute-start.2 = (bf16[128,1024]{1,0:T(8,128)(2,1)S(1)}, bf16[128,1024]{1,0:T(8,128)(2,1)}, u32[]{:S(2)}, u32[]{:S(2)}) collective-permute-start(bf16[128,1024]{1,0:T(8,128)(2,1)S(1)} %collective-permute-done.1), channel_id=1, source_target_pairs={{0,4},{4,8},{8,12},{12,16},{16,20},{20,24},{24,28},{28,0},{1,5},{5... | collective-permute-start | bytes 786440 | tf_op jit(solution)/shard_map/ppermute | solution.py:26
  148.0 12.4 %collective-permute-start.5 = (bf16[128,1024]{1,0:T(8,128)(2,1)S(1)}, bf16[128,1024]{1,0:T(8,128)(2,1)}, u32[]{:S(2)}, u32[]{:S(2)}) collective-permute-start(bf16[128,1024]{1,0:T(8,128)(2,1)S(1)} %collective-permute-done.4), channel_id=1, source_target_pairs={{4,0},{8,4},{12,8},{16,12},{20,16},{24,20},{28,24},{0,28},{5,1},{9... | collective-permute-start | bytes 786440 | tf_op jit(solution)/shard_map/ppermute | solution.py:28
  157.7 12.3 %collective-permute-start.3 = (bf16[128,1024]{1,0:T(8,128)(2,1)}, bf16[128,1024]{1,0:T(8,128)(2,1)}, u32[]{:S(2)}, u32[]{:S(2)}) collective-permute-start(bf16[128,1024]{1,0:T(8,128)(2,1)} %collective-permute-done.2), channel_id=1, source_target_pairs={{0,4},{4,8},{8,12},{12,16},{16,20},{20,24},{24,28},{28,0},{1,5},{5... | collective-permute-start | bytes 786440 | tf_op jit(solution)/shard_map/ppermute | solution.py:26
  160.3 18.5 %collective-permute-start.6 = (bf16[128,1024]{1,0:T(8,128)(2,1)}, bf16[128,1024]{1,0:T(8,128)(2,1)S(1)}, u32[]{:S(2)}, u32[]{:S(2)}) collective-permute-start(bf16[128,1024]{1,0:T(8,128)(2,1)} %collective-permute-done.5), channel_id=1, source_target_pairs={{4,0},{8,4},{12,8},{16,12},{20,16},{24,20},{28,24},{0,28},{5,1},{9... | collective-permute-start | bytes 786440 | tf_op jit(solution)/shard_map/ppermute | solution.py:28
  183.2 95.4 %copy-start.30 = (f32[1024]{0:T(1024)S(1)}, f32[1024]{0:T(1024)}, u32[]{:S(2)}) copy-start(f32[1024]{0:T(1024)} %param.26) | copy-start | bytes 12292
  311.4 285.9 %reduce-scatter.15.cloned.1.call-start = ((), (), s32[]{:S(2)}) async-start(), calls=%async_computation.11 | async-start | bytes 2359296
  324.8 283.2 %reduce-scatter.11.cloned.1.call-start = ((), (), s32[]{:S(2)}) async-start(), calls=%async_computation.9 | async-start | bytes 2359296 | tf_op jit(solution)/shard_map/reduce_scatter | solution.py:234
  324.9 141.5 %copy-start.18 = (f32[2070]{0:T(1024)}, f32[2070]{0:T(1024)S(1)}, u32[]{:S(2)}) copy-start(f32[2070]{0:T(1024)S(1)} %fusion.77) | copy-start | bytes 24844
  337.1 335.2 %reduce-scatter.13.cloned.1.call-start = ((), (), s32[]{:S(2)}) async-start(), calls=%async_computation.10 | async-start | bytes 589824
  466.4 17.4 %slice-start = ((s8[4243456]{0:T(1024)(128)(4,1)}), s8[4194304]{0:T(1024)(128)(4,1)S(1)}, s32[]{:S(2)}) async-start(s8[4243456]{0:T(1024)(128)(4,1)} %bitcast.156), calls=%async_computation.13 | async-start | bytes 8388608
  571.0 169.6 %reduce-scatter.9.cloned.1.call-start = ((), (), s32[]{:S(2)}) async-start(), calls=%async_computation.8 | async-start | bytes 1769472 | tf_op jit(solution)/shard_map/reduce_scatter | solution.py:228
  582.6 315.4 %all-reduce.11.cloned.1.call-start = ((), (), s32[]{:S(2)}) async-start(), calls=%async_computation.12 | async-start | bytes 16973824 | tf_op jit(solution)/shard_map/psum | solution.py:174
  903.4 27.7 %slice-start.2 = ((s8[4243456]{0:T(1024)(128)(4,1)}), s8[49152]{0:T(1024)(128)(4,1)S(1)}, s32[]{:S(2)}) async-start(s8[4243456]{0:T(1024)(128)(4,1)} %bitcast.159), calls=%async_computation.15 | async-start | bytes 98304
  (34 other events, 214.8 us)
Sparse Core Ops, SparseCore 0:
  10.8 49.9 all-gather.2
  63.4 50.3 all-gather.4
  124.5 154.0 all-reduce.6
  311.6 154.8 all-reduce.8
  469.8 67.8 reduce-scatter.14
  541.1 66.8 reduce-scatter.10
  611.4 60.8 reduce-scatter.12
  676.1 64.4 reduce-scatter.8
  743.8 154.1 all-reduce.10
